TPU v7x, 128 devices: a whole 4x4x4 slice. The times are simulated.
128 devices in a mesh: mesh: 16 (over z, x), bg: 8 (over y, core).
Axes of the slice: x: 4, y: 4, z: 4, core: 2. Of those that a mesh axis runs over, the one named last changes fastest.
Arguments:
- displacement: float32 [3, 64, 32, 128], P(None, 'mesh', 'bg'), may hold values from -0.4 to 0.4
- bg_coef: float32 [8, 2097152], P(None, ('mesh', 'bg')), may hold values from -0.3 to 0.3
- query_elem: int32 [128, 128, 136], P(('mesh', 'bg')), may hold values from 0 to 16383
- query_point: int32 [128, 128, 136], P(('mesh', 'bg')), may hold values from 0 to 6912, as said below
- query_coord: float32 [128, 128, 3, 136], P(('mesh', 'bg')), may hold values from 0 to 1
Outputs:
- new_displacement: float32 [3, 64, 32, 128], P(None, 'mesh', 'bg')
- line_coeffs: float32 [2, 5], replicated
Inputs may be any that keep to these rules, and one draw needn't show every extreme that they name: `query_point`: in each row every quadrature point 0 to 6911 of the row's device fills exactly one slot; all other slots hold 6912 and are empty. In every draw some owner's bucket is full in every row.
All inputs are finite; a program needn't handle non-finite values.
Results may differ from a plain program's by a relative error of at most 0.0003.
Values sent between devices are 32-bit elements; how exact they have to be, the bound alone decides.
No kernel may reach another device: no remote copies, remote signals or barrier semaphores. Data moves between devices by JAX's collectives and lax.ppermute only.
A program may use at most 64 MiB of HBM per device.

v0:
```python
import jax
import jax.numpy as jnp
import numpy as np
from jax import lax
from jax.sharding import PartitionSpec as P

PASSES = 2
LS_STEPS = 4
GAUSS_POINTS = np.array([0.5 - 0.5 * np.sqrt(0.6), 0.5, 0.5 + 0.5 * np.sqrt(0.6)])
GAUSS_WEIGHTS = np.array([5.0 / 18.0, 8.0 / 18.0, 5.0 / 18.0])


def extended(block, sides, width):
    for axis, dim in sides:
        count = lax.axis_size(axis)
        forward = [(i, i + 1) for i in range(count - 1)]
        forward.append((count - 1, 0))
        backward = [(target, source) for source, target in forward]
        low = lax.ppermute(
            lax.slice_in_dim(block, block.shape[dim] - width, None, axis=dim), axis, forward
        )
        high = lax.ppermute(lax.slice_in_dim(block, 0, width, axis=dim), axis, backward)
        block = jnp.concatenate([low, block, high], axis=dim)
    return block


def basis_tables(elements, periodic):
    node_count = 2 * elements if periodic else 2 * elements + 1
    values = np.zeros((node_count, 3 * elements))
    slopes = np.zeros((node_count, 3 * elements))
    points = GAUSS_POINTS
    shape_values = [
        2.0 * (points - 0.5) * (points - 1.0),
        -4.0 * points * (points - 1.0),
        2.0 * points * (points - 0.5),
    ]
    shape_slopes = [4.0 * points - 3.0, 4.0 - 8.0 * points, 4.0 * points - 1.0]
    for offset in range(3):
        node_rows = (2 * np.arange(elements) + offset) % node_count
        for gauss_index in range(3):
            columns = 3 * np.arange(elements) + gauss_index
            values[node_rows, columns] += shape_values[offset][gauss_index]
            slopes[node_rows, columns] += shape_slopes[offset][gauss_index]
    return (jnp.asarray(values, dtype=jnp.float32), jnp.asarray(slopes, dtype=jnp.float32))


def quad_weights(z_elems, y_elems, x_elems):
    along_z = jnp.asarray(np.tile(GAUSS_WEIGHTS, z_elems), dtype=jnp.float32)
    along_y = jnp.asarray(np.tile(GAUSS_WEIGHTS, y_elems), dtype=jnp.float32)
    along_x = jnp.asarray(np.tile(GAUSS_WEIGHTS, x_elems), dtype=jnp.float32)
    return along_z[:, None, None] * along_y[None, :, None] * along_x[None, None, :]


def gradients(node_field, tables):
    z_value, z_slope, y_value, y_slope, value_along_x, x_slope = tables
    highest = lax.Precision.HIGHEST
    value_z = jnp.einsum("czyx,zk->ckyx", node_field, z_value, precision=highest)
    slope_z = jnp.einsum("czyx,zk->ckyx", node_field, z_slope, precision=highest)
    value_zy = jnp.einsum("ckyx,yl->cklx", value_z, y_value, precision=highest)
    slope_y = jnp.einsum("ckyx,yl->cklx", value_z, y_slope, precision=highest)
    slope_zy = jnp.einsum("ckyx,yl->cklx", slope_z, y_value, precision=highest)
    deriv_x = jnp.einsum("cklx,xm->cklm", value_zy, x_slope, precision=highest)
    deriv_y = jnp.einsum("cklx,xm->cklm", slope_y, value_along_x, precision=highest)
    deriv_z = jnp.einsum("cklx,xm->cklm", slope_zy, value_along_x, precision=highest)
    return jnp.stack([deriv_x, deriv_y, deriv_z], axis=1)


def identity_block():
    return jnp.eye(3, dtype=jnp.float32)[:, :, None, None, None]


def gram(left_part, right_part):
    return jnp.sum(left_part[:, :, None] * right_part[:, None, :], axis=0)


def energy(node_field, tables, target_size_scale, weights):
    jacobian = gradients(node_field, tables) + identity_block()
    strain = gram(jacobian, jacobian) * target_size_scale - identity_block()
    return jnp.sum(weights * jnp.sum(strain * strain, axis=(0, 1)))


def line_terms(node_field, direction, tables, target_size_scale, weights):
    jacobian = gradients(node_field, tables) + identity_block()
    motion = gradients(direction, tables)
    strain_zero = gram(jacobian, jacobian) * target_size_scale - identity_block()
    mixed = gram(jacobian, motion)
    strain_one = (mixed + jnp.swapaxes(mixed, 0, 1)) * target_size_scale
    strain_two = gram(motion, motion) * target_size_scale

    def weighted(first_part, latter_portion):
        return jnp.sum(weights * jnp.sum(first_part * latter_portion, axis=(0, 1)))

    zero_zero = weighted(strain_zero, strain_zero)
    zero_one = weighted(strain_zero, strain_one)
    zero_two = weighted(strain_zero, strain_two)
    one_two = weighted(strain_one, strain_two)
    two_two = weighted(strain_two, strain_two)
    gauss_newton = weighted(strain_one, strain_one)
    return (
        zero_zero,
        2.0 * zero_one,
        gauss_newton + 2.0 * zero_two,
        2.0 * one_two,
        two_two,
        gauss_newton,
    )


def line_search(terms):
    const_term, linear, quadratic, cubic_term, quartic, gauss_newton = terms
    step_len = jnp.zeros((), jnp.float32)
    for search_turn in range(LS_STEPS):
        slope = linear + step_len * (
            2.0 * quadratic + step_len * (3.0 * cubic_term + step_len * 4.0 * quartic)
        )
        curvature = 2.0 * quadratic + step_len * (6.0 * cubic_term + step_len * 12.0 * quartic)
        step_len = step_len - slope / jnp.maximum(curvature, gauss_newton + 1e-06)
    return step_len


def inverse_square(coefs, coords):
    along_x = coords[:, 0]
    along_y = coords[:, 1]
    along_z = coords[:, 2]
    summed = jnp.zeros_like(along_x)
    for corner in range(8):
        weight_x = along_x if corner & 1 else 1.0 - along_x
        weight_y = along_y if corner & 2 else 1.0 - along_y
        weight_z = along_z if corner & 4 else 1.0 - along_z
        summed = summed + weight_x * weight_y * weight_z * coefs[:, corner]
    return jnp.exp(-2.0 * summed)


def gather_coefs(table, elem_ids):
    index_rows = elem_ids[:, 0, :]
    corner_rows = jnp.take(jnp.transpose(table), index_rows, axis=0)
    return jnp.moveaxis(corner_rows, 2, 1)


def answer(reply):
    return lax.all_to_all(reply, ("mesh", "bg"), split_axis=0, concat_axis=0, tiled=True)


def assemble(local_part):
    padded_z = extended(local_part, (("mesh", 1),), 1)
    partial_sum = local_part.at[:, 0].add(padded_z[:, 0]).at[:, -1].add(padded_z[:, -1])
    padded_y = extended(partial_sum, (("bg", 2),), 1)
    summed = partial_sum.at[:, :, 0].add(padded_y[:, :, 0]).at[:, :, -1].add(padded_y[:, :, -1])
    return summed


def shards(displacement, bg_coef, query_elem, query_point, query_coord):
    devices = lax.axis_size("mesh") * lax.axis_size("bg")
    z_elems = displacement.shape[1] // 2
    y_elems = displacement.shape[2] // 2
    x_elems = displacement.shape[3] // 2
    tables = (
        basis_tables(z_elems, False) + basis_tables(y_elems, False) + basis_tables(x_elems, True)
    )
    weights = quad_weights(z_elems, y_elems, x_elems)
    point_count = 27 * z_elems * y_elems * x_elems
    elem_ids = query_elem.reshape(devices, 1, -1)
    coords = query_coord.reshape(devices, 3, -1)
    fetched = answer(
        gather_coefs(
            bg_coef,
            lax.all_to_all(elem_ids, ("mesh", "bg"), split_axis=0, concat_axis=0, tiled=True),
        )
    )
    found_vals = inverse_square(fetched, coords).reshape(-1)
    target_size_scale = (
        jnp.zeros((point_count,), jnp.float32)
        .at[query_point.reshape(-1)]
        .set(found_vals, mode="drop")
    )
    target_size_scale = target_size_scale.reshape(3 * z_elems, 3 * y_elems, 3 * x_elems)

    def local_energy(values):
        return energy(values, tables, target_size_scale, weights)

    node_field = assemble(jnp.pad(displacement, ((0, 0), (0, 1), (0, 1), (0, 0))))
    history = []
    for newton_pass in range(PASSES):
        direction = -assemble(jax.grad(local_energy)(node_field))
        partial_terms = jnp.stack(
            line_terms(node_field, direction, tables, target_size_scale, weights)
        )
        totals = lax.psum(partial_terms, ("mesh", "bg"))
        step_len = line_search(totals)
        node_field = node_field + step_len * direction
        history.append(totals[:5] / (devices * z_elems * y_elems * x_elems))
    return (node_field[:, :-1, :-1], jnp.stack(history))


def solution(mesh):
    in_specs = (
        P(None, "mesh", "bg", None),
        P(None, ("mesh", "bg")),
        P(("mesh", "bg"), None, None),
        P(("mesh", "bg"), None, None),
        P(("mesh", "bg"), None, None, None),
    )
    out_specs = (P(None, "mesh", "bg", None), P())
    return jax.shard_map(shards, mesh=mesh, in_specs=in_specs, out_specs=out_specs, check_vma=False)
```

profile of v0, /device:TPU:1, one launch (start us, length us, event | category | flops | bytes accessed | tf_op | source)
XLA Modules:
  0.0 415.2 jit_solution(10419066818697922350)
XLA Ops:
  0.7 2.1 collective-permute-start
  2.8 1.6 copy.164
  4.4 10.7 %all-to-all-start = ((s32[128,1,136]{2,1,0:T(1,128)}), s32[128,1,136]{2,1,0:T(1,128)S(1)}, u32[]{:S(2)}, u32[]{:S(2)}) async-start(s32[128,1,136]{2,1,0:T(1,128)} %bitcast.21), calls=%async_computation | async-start | bytes 262144 | tf_op jit(solution)/shard_map/all_to_all | solution.py:167
  15.1 1.0 copy.160
  16.2 0.7 compare_select_fusion.1
  16.9 1.0 fusion.53
  18.0 5.5 %collective-permute-start.1 = (f32[3,1,5,128]{3,1,2,0:T(1,128)S(1)}, f32[3,1,5,128]{3,1,2,0:T(1,128)S(1)}, u32[]{:S(2)}, u32[]{:S(2)}) collective-permute-start(f32[3,1,5,128]{3,1,2,0:T(1,128)S(1)} %get-tuple-element.209), channel_id=1, source_target_pairs={{8,0},{16,8},{24,16},{32,24},{40,32},{48,40},{56,48},{64,56},{72,6... | collective-permute-start | bytes 23048 | tf_op jit(solution)/shard_map/ppermute | solution.py:22
  23.5 0.7 collective-permute-done.1
  24.3 2.4 collective-permute-start.2
  26.8 0.8 collective-permute-done.2
  27.5 2.4 collective-permute-start.3
  29.9 5.3 %copy.167 = f32[8,16384]{0,1:T(8,128)} copy(f32[8,16384]{1,0:T(8,128)S(1)} %copy-done.4) | data formatting | bytes 1048576 | tf_op args[1]
  36.9 0.3 convolution_bitcast_fusion.9
  37.3 0.4 fusion.8
  37.8 61.3 %gather_fusion = f32[17408,8]{1,0:T(8,128)} fusion(f32[16384,8]{1,0:T(8,128)} %bitcast.265, s32[17408]{0:T(1024)S(1)} %broadcast_clamp_fusion), kind=kCustom, calls=%fused_computation | custom fusion | bytes 1183744 | tf_op jit(solution)/shard_map/jit(_take)/gather | solution.py:136
  99.1 6.7 %copy.168 = f32[128,136,8]{1,2,0:T(8,128)S(1)} copy(f32[128,136,8]{2,1,0:T(8,128)} %bitcast.266) | data formatting | bytes 1114112 | tf_op jit(solution)/shard_map/jit(_take)/gather | solution.py:136
  106.1 1.1 select_bitcast_fusion
  107.2 7.9 %all-to-all-start.1 = ((f32[128,8,136]{2,1,0:T(8,128)}), f32[128,8,136]{2,1,0:T(8,128)S(1)}, u32[]{:S(2)}, u32[]{:S(2)}) async-start(f32[128,8,136]{2,1,0:T(8,128)} %select_bitcast_fusion), calls=%async_computation.1 | async-start | bytes 2097152 | tf_op jit(solution)/shard_map/all_to_all | solution.py:141
  115.1 0.3 convolution_bitcast_fusion.10
  115.5 0.3 convolution_bitcast_fusion.11
  115.8 0.4 multiply_reduce_fusion.9
  116.3 17.6 %all-to-all-done.1 = f32[128,8,136]{2,1,0:T(8,128)S(1)} async-done(((f32[128,8,136]{2,1,0:T(8,128)}), f32[128,8,136]{2,1,0:T(8,128)S(1)}, u32[]{:S(2)}, u32[]{:S(2)}) %all-to-all-start.1) | async-done | bytes 557088 | tf_op jit(solution)/shard_map/all_to_all | solution.py:141
  133.9 2.9 slice_reduce_fusion.6
  137.9 64.3 %scatter_custom_fusion = f32[6912]{0:T(1024)S(1)} fusion(s32[17408]{0:T(1024)} %bitcast.268, f32[17408]{0:T(1024)S(1)} %multiply_exponential_fusion, f32[]{:T(128)} %constant.313.clone.1), kind=kCustom, calls=%fused_computation.166 | custom fusion | bytes 28160 | tf_op jit(solution)/shard_map/scatter | solution.py:174
  202.3 0.5 multiply_reduce_fusion.8
  205.1 0.5 collective-permute-start.4
  205.6 5.3 %collective-permute-done.4 = f32[3,1,5,128]{3,1,2,0:T(1,128)S(1)} collective-permute-done((f32[3,1,5,128]{3,1,2,0:T(1,128)S(1)}, f32[3,1,5,128]{3,1,2,0:T(1,128)S(1)}, u32[]{:S(2)}, u32[]{:S(2)}) %collective-permute-start.4) | collective-permute-done | bytes 7712 | tf_op jit(solution)/shard_map/ppermute | solution.py:19
  211.1 2.4 collective-permute-done.5
  213.7 3.6 collective-permute-start.6
  217.3 0.8 collective-permute-done.6
  218.1 3.5 collective-permute-start.7
  221.7 0.8 collective-permute-done.7
  223.5 0.3 convolution_bitcast_fusion.6
  223.8 0.3 convolution_bitcast_fusion.7
  224.2 0.3 convolution_bitcast_fusion.8
  224.5 0.7 multiply_reduce_fusion.5
  225.2 0.4 multiply_reduce_fusion.18
  225.6 0.8 fusion.37
  228.9 2.0 stack.121
  230.9 65.5 %psum.14 = f32[6]{0:T(128)S(1)} all-reduce(f32[6]{0:T(128)S(1)} %stack.121), channel_id=1, replica_groups=mesh['mesh'=16,'bg'=8] {'mesh','bg'}, use_global_device_ids=true, to_apply=%region_18.19 | all-reduce | flops 6 | bytes 48 | tf_op jit(solution)/shard_map/psum | solution.py:188
  296.4 0.7 fusion.60
  308.1 0.3 convolution_bitcast_fusion.3
  308.5 0.3 convolution_bitcast_fusion.4
  308.8 0.3 convolution_bitcast_fusion.5
  309.2 0.4 multiply_reduce_fusion.4
  309.7 0.5 multiply_reduce_fusion.3
  310.8 0.3 convolution_bitcast_fusion.15
  312.5 5.8 %collective-permute-done.8 = f32[3,1,5,128]{3,1,2,0:T(1,128)S(1)} collective-permute-done((f32[3,1,5,128]{3,1,2,0:T(1,128)S(1)}, f32[3,1,5,128]{3,1,2,0:T(1,128)S(1)}, u32[]{:S(2)}, u32[]{:S(2)}) %collective-permute-start.8) | collective-permute-done | bytes 7712 | tf_op jit(solution)/shard_map/ppermute | solution.py:19
  318.5 2.4 collective-permute-done.9
  321.0 1.8 collective-permute-start.10
  322.8 2.2 collective-permute-done.10
  325.1 3.7 collective-permute-start.11
  328.7 0.8 collective-permute-done.11
  330.6 0.3 convolution_bitcast_fusion
  330.9 0.3 convolution_bitcast_fusion.1
  331.3 0.3 convolution_bitcast_fusion.2
  331.6 0.7 multiply_reduce_fusion
  332.3 0.4 multiply_reduce_fusion.12
  332.6 0.8 fusion.43
  336.0 2.0 stack.136
  338.0 65.3 %psum.15 = f32[6]{0:T(128)S(1)} all-reduce(f32[6]{0:T(128)S(1)} %stack.136), channel_id=1, replica_groups=mesh['mesh'=16,'bg'=8] {'mesh','bg'}, use_global_device_ids=true, to_apply=%region_36.37 | all-reduce | flops 6 | bytes 48 | tf_op jit(solution)/shard_map/psum | solution.py:188
  403.3 0.7 fusion.59
  414.0 0.6 copy.210
  414.6 0.6 pad_maximum_fusion.2
  (117 shorter events, 11.3 us)
Async XLA Ops:
  0.6 22.8 %copy-start.7 = (f32[6]{0:T(128)S(1)}, f32[6]{0:T(128)}, u32[]{:S(2)}) copy-start(f32[6]{0:T(128)} %constant.334.clone) | copy-start | bytes 76
  0.6 26.0 %copy-start.6 = (f32[192]{0:T(256)S(1)}, f32[192]{0:T(256)}, u32[]{:S(2)}) copy-start(f32[192]{0:T(256)} %constant.335.clone) | copy-start | bytes 2308
  0.7 17.2 %copy-start.5 = (f32[3,4,4,128]{3,2,1,0:T(4,128)S(1)}, f32[3,4,4,128]{3,2,1,0:T(4,128)}, u32[]{:S(2)}) copy-start(f32[3,4,4,128]{3,2,1,0:T(4,128)} %param.38) | copy-start | bytes 73732
  0.7 29.2 %copy-start.4 = (f32[8,16384]{1,0:T(8,128)S(1)}, f32[8,16384]{1,0:T(8,128)}, u32[]{:S(2)}) copy-start(f32[8,16384]{1,0:T(8,128)} %param.39) | copy-start | bytes 1572868
  0.7 17.2 %collective-permute-start = (f32[3,1,5,128]{3,1,2,0:T(1,128)S(1)}, f32[3,1,5,128]{3,1,2,0:T(1,128)S(1)}, u32[]{:S(2)}, u32[]{:S(2)}) collective-permute-start(f32[3,1,5,128]{3,1,2,0:T(1,128)S(1)} %slice.391), channel_id=1, source_target_pairs={{0,8},{8,16},{16,24},{24,32},{32,40},{40,48},{48,56},{56,64},{64,7... | collective-permute-start | bytes 23048 | tf_op jit(solution)/shard_map/ppermute | solution.py:19
  4.4 32.8 %all-to-all-start = ((s32[128,1,136]{2,1,0:T(1,128)}), s32[128,1,136]{2,1,0:T(1,128)S(1)}, u32[]{:S(2)}, u32[]{:S(2)}) async-start(s32[128,1,136]{2,1,0:T(1,128)} %bitcast.21), calls=%async_computation | async-start | bytes 262144 | tf_op jit(solution)/shard_map/all_to_all | solution.py:167
  18.0 6.2 %collective-permute-start.1 = (f32[3,1,5,128]{3,1,2,0:T(1,128)S(1)}, f32[3,1,5,128]{3,1,2,0:T(1,128)S(1)}, u32[]{:S(2)}, u32[]{:S(2)}) collective-permute-start(f32[3,1,5,128]{3,1,2,0:T(1,128)S(1)} %get-tuple-element.209), channel_id=1, source_target_pairs={{8,0},{16,8},{24,16},{32,24},{40,32},{48,40},{56,48},{64,56},{72,6... | collective-permute-start | bytes 23048 | tf_op jit(solution)/shard_map/ppermute | solution.py:22
  24.3 3.2 collective-permute-start.2
  27.5 8.3 %collective-permute-start.3 = (f32[3,5,1,128]{3,1,2,0:T(8,128)S(1)}, f32[3,5,1,128]{3,1,2,0:T(8,128)S(1)}, u32[]{:S(2)}, u32[]{:S(2)}) collective-permute-start(f32[3,5,1,128]{3,1,2,0:T(8,128)S(1)} %get-tuple-element.207), channel_id=1, source_target_pairs={{1,0},{2,1},{3,2},{4,3},{5,4},{6,5},{7,6},{0,7},{9,8},{10,9},{11,1... | collective-permute-start | bytes 23048 | tf_op jit(solution)/shard_map/ppermute | solution.py:22
  29.9 6.0 %copy-start.3 = (f32[5,6,1,1]{0,1,3,2:T(8,128)S(1)}, f32[5,6,1,1]{0,1,3,2:T(8,128)}, u32[]{:S(2)}) copy-start(f32[5,6,1,1]{0,1,3,2:T(8,128)} %constant.344) | copy-start | bytes 364
  35.2 0.9 copy-start.2
  35.2 1.7 copy-start
  107.2 8.3 %copy-start.1 = (f32[128,192,1,1]{0,1,3,2:T(8,128)S(1)}, f32[128,192,1,1]{0,1,3,2:T(8,128)}, u32[]{:S(2)}) copy-start(f32[128,192,1,1]{0,1,3,2:T(8,128)} %constant.343) | copy-start | bytes 294916
  107.2 26.7 %all-to-all-start.1 = ((f32[128,8,136]{2,1,0:T(8,128)}), f32[128,8,136]{2,1,0:T(8,128)S(1)}, u32[]{:S(2)}, u32[]{:S(2)}) async-start(f32[128,8,136]{2,1,0:T(8,128)} %select_bitcast_fusion), calls=%async_computation.1 | async-start | bytes 2097152 | tf_op jit(solution)/shard_map/all_to_all | solution.py:141
  205.1 5.9 %collective-permute-start.4 = (f32[3,1,5,128]{3,1,2,0:T(1,128)S(1)}, f32[3,1,5,128]{3,1,2,0:T(1,128)S(1)}, u32[]{:S(2)}, u32[]{:S(2)}) collective-permute-start(f32[3,1,5,128]{3,1,2,0:T(1,128)S(1)} %slice.440), channel_id=1, source_target_pairs={{0,8},{8,16},{16,24},{24,32},{32,40},{40,48},{48,56},{56,64},{64,7... | collective-permute-start | bytes 23048 | tf_op jit(solution)/shard_map/ppermute | solution.py:19
  211.0 2.6 collective-permute-start.5
  213.7 4.5 %collective-permute-start.6 = (f32[3,5,1,128]{3,1,2,0:T(8,128)S(1)}, f32[3,5,1,128]{3,1,2,0:T(8,128)S(1)}, u32[]{:S(2)}, u32[]{:S(2)}) collective-permute-start(f32[3,5,1,128]{3,1,2,0:T(8,128)S(1)} %slice.443), channel_id=1, source_target_pairs={{0,1},{1,2},{2,3},{3,4},{4,5},{5,6},{6,7},{7,0},{8,9},{9,10},{10,1... | collective-permute-start | bytes 23048 | tf_op jit(solution)/shard_map/ppermute | solution.py:19
  218.1 4.3 %collective-permute-start.7 = (f32[3,5,1,128]{3,1,2,0:T(8,128)S(1)}, f32[3,5,1,128]{3,1,2,0:T(8,128)S(1)}, u32[]{:S(2)}, u32[]{:S(2)}) collective-permute-start(f32[3,5,1,128]{3,1,2,0:T(8,128)S(1)} %get-tuple-element.203), channel_id=1, source_target_pairs={{1,0},{2,1},{3,2},{4,3},{5,4},{6,5},{7,6},{0,7},{9,8},{10,9},{11,1... | collective-permute-start | bytes 23048 | tf_op jit(solution)/shard_map/ppermute | solution.py:22
  312.4 5.9 %collective-permute-start.8 = (f32[3,1,5,128]{3,1,2,0:T(1,128)S(1)}, f32[3,1,5,128]{3,1,2,0:T(1,128)S(1)}, u32[]{:S(2)}, u32[]{:S(2)}) collective-permute-start(f32[3,1,5,128]{3,1,2,0:T(1,128)S(1)} %slice.446), channel_id=1, source_target_pairs={{0,8},{8,16},{16,24},{24,32},{32,40},{40,48},{48,56},{56,64},{64,7... | collective-permute-start | bytes 23048 | tf_op jit(solution)/shard_map/ppermute | solution.py:19
  318.3 2.6 collective-permute-start.9
  321.0 4.1 collective-permute-start.10
  325.1 4.5 %collective-permute-start.11 = (f32[3,5,1,128]{3,1,2,0:T(8,128)S(1)}, f32[3,5,1,128]{3,1,2,0:T(8,128)S(1)}, u32[]{:S(2)}, u32[]{:S(2)}) collective-permute-start(f32[3,5,1,128]{3,1,2,0:T(8,128)S(1)} %get-tuple-element.199), channel_id=1, source_target_pairs={{1,0},{2,1},{3,2},{4,3},{5,4},{6,5},{7,6},{0,7},{9,8},{10,9},{11,1... | collective-permute-start | bytes 23048 | tf_op jit(solution)/shard_map/ppermute | solution.py:22
where the time goes:
time: 416 us; the launch traced here: 415 us
  local copies, waits for them, and re-layouts  153 us (37%)
  blocking collectives  131 us (31%)
  starting transfers between devices  44.3 us (11%)
  waiting for transfers between devices  39.7 us (10%)
  between operations  26.7 us (6%)
  matrix products  12.1 us (3%)
  other arithmetic  9.06 us (2%)
    psum x2, blocking collectives, shards(): totals = lax.psum(partial_terms, ('mesh', 'bg'))  131 us
    gather x2, local copies, waits for them, and re-layouts, gather_coefs(): corner_rows = jnp.take(jnp.transpose(table), index_rows, axis=0)  68 us
    scatter x1, local copies, waits for them, and re-layouts, shards(): target_size_scale = jnp.zeros((point_count,), jnp.float32).at[query_point...  64.3 us
    all_to_all x1, waiting for transfers between devices, answer(): lax.all_to_all(reply, ('mesh', 'bg'), split_axis=0, concat_axis=0, tiled=...  17.6 us
    ppermute x6, starting transfers between devices, extended(): lax.ppermute(lax.slice_in_dim(block, 0, width, axis=dim), axis, backward)  15.1 us
    ppermute x6, waiting for transfers between devices, extended(): lax.ppermute(lax.slice_in_dim(block, block.shape[dim] - width, None, axis...  15 us
    all_to_all x1, starting transfers between devices, shards(): lax.all_to_all(elem_ids, ('mesh', 'bg'), split_axis=0, concat_axis=0, til...  10.7 us
    ppermute x6, starting transfers between devices, extended(): lax.ppermute(lax.slice_in_dim(block, block.shape[dim] - width, None, axis...  10.6 us
  transfers between devices with their start and end apart: 14, of which 11 were waited for; matrix products, arithmetic and copies ran while one was open for 3% of the time, Pallas kernels for 0%

commit v1 on v0

--- a/solution.py
+++ b/solution.py
@@ -185,7 +185,7 @@
         partial_terms = jnp.stack(
             line_terms(node_field, direction, tables, target_size_scale, weights)
         )
-        totals = lax.psum(partial_terms, ("mesh", "bg"))
+        totals = lax.psum(lax.psum(partial_terms, "bg"), "mesh")
         step_len = line_search(totals)
         node_field = node_field + step_len * direction
         history.append(totals[:5] / (devices * z_elems * y_elems * x_elems))

time: 416 us -> 392 us (0.942)
  the two profiles are of different devices: /device:TPU:1 before, /device:TPU:0 now
where the time goes in v1:
time: 392 us; the launch traced here: 391 us
  local copies, waits for them, and re-layouts  153 us (39%)
  blocking collectives  108 us (28%)
  waiting for transfers between devices  55 us (14%)
  starting transfers between devices  27.7 us (7%)
  between operations  26.7 us (7%)
  matrix products  12.1 us (3%)
  other arithmetic  9.06 us (2%)
    psum x4, blocking collectives, shards(): totals = lax.psum(lax.psum(partial_terms, 'bg'), 'mesh')  108 us
    gather x2, local copies, waits for them, and re-layouts, gather_coefs(): corner_rows = jnp.take(jnp.transpose(table), index_rows, axis=0)  68 us
    scatter x1, local copies, waits for them, and re-layouts, shards(): target_size_scale = jnp.zeros((point_count,), jnp.float32).at[query_point...  64.3 us
    ppermute x6, waiting for transfers between devices, extended(): lax.ppermute(lax.slice_in_dim(block, block.shape[dim] - width, None, axis...  26.1 us
    all_to_all x1, waiting for transfers between devices, answer(): lax.all_to_all(reply, ('mesh', 'bg'), split_axis=0, concat_axis=0, tiled=...  17.7 us
    ppermute x6, waiting for transfers between devices, extended(): lax.ppermute(lax.slice_in_dim(block, 0, width, axis=dim), axis, backward)  11.2 us
    all_to_all x1, starting transfers between devices, shards(): lax.all_to_all(elem_ids, ('mesh', 'bg'), split_axis=0, concat_axis=0, til...  10.8 us
    all_to_all x1, starting transfers between devices, answer(): lax.all_to_all(reply, ('mesh', 'bg'), split_axis=0, concat_axis=0, tiled=...  9.14 us
  transfers between devices with their start and end apart: 14, of which 11 were waited for; matrix products, arithmetic and copies ran while one was open for 3% of the time, Pallas kernels for 0%

profile of v1, /device:TPU:0, one launch (start us, length us, event | category | flops | bytes accessed | tf_op | source)
XLA Modules:
  0.0 391.4 jit_solution(6061046410397599413)
XLA Ops:
  0.7 1.7 collective-permute-start
  2.4 1.6 copy.164
  4.0 10.8 %all-to-all-start = ((s32[128,1,136]{2,1,0:T(1,128)}), s32[128,1,136]{2,1,0:T(1,128)S(1)}, u32[]{:S(2)}, u32[]{:S(2)}) async-start(s32[128,1,136]{2,1,0:T(1,128)} %bitcast.21), calls=%async_computation | async-start | bytes 262144 | tf_op jit(solution)/shard_map/all_to_all | solution.py:167
  14.8 1.0 copy.160
  15.9 0.7 compare_select_fusion.1
  16.6 1.0 fusion.53
  17.6 5.1 %collective-permute-start.1 = (f32[3,1,5,128]{3,1,2,0:T(1,128)S(1)}, f32[3,1,5,128]{3,1,2,0:T(1,128)S(1)}, u32[]{:S(2)}, u32[]{:S(2)}) collective-permute-start(f32[3,1,5,128]{3,1,2,0:T(1,128)S(1)} %get-tuple-element.209), channel_id=1, source_target_pairs={{8,0},{16,8},{24,16},{32,24},{40,32},{48,40},{56,48},{64,56},{72,6... | collective-permute-start | bytes 23048 | tf_op jit(solution)/shard_map/ppermute | solution.py:22
  22.8 1.2 collective-permute-done.1
  24.3 4.2 %collective-permute-done.2 = f32[3,5,1,128]{3,1,2,0:T(8,128)S(1)} collective-permute-done((f32[3,5,1,128]{3,1,2,0:T(8,128)S(1)}, f32[3,5,1,128]{3,1,2,0:T(8,128)S(1)}, u32[]{:S(2)}, u32[]{:S(2)}) %collective-permute-start.2) | collective-permute-done | bytes 7712 | tf_op jit(solution)/shard_map/ppermute | solution.py:19
  28.5 5.3 %copy.167 = f32[8,16384]{0,1:T(8,128)} copy(f32[8,16384]{1,0:T(8,128)S(1)} %copy-done.4) | data formatting | bytes 1048576 | tf_op args[1]
  35.5 0.3 convolution_bitcast_fusion.9
  35.9 0.4 fusion.8
  36.5 61.3 %gather_fusion = f32[17408,8]{1,0:T(8,128)} fusion(f32[16384,8]{1,0:T(8,128)} %bitcast.265, s32[17408]{0:T(1024)S(1)} %broadcast_clamp_fusion), kind=kCustom, calls=%fused_computation | custom fusion | bytes 1183744 | tf_op jit(solution)/shard_map/jit(_take)/gather | solution.py:136
  97.7 6.7 %copy.168 = f32[128,136,8]{1,2,0:T(8,128)S(1)} copy(f32[128,136,8]{2,1,0:T(8,128)} %bitcast.266) | data formatting | bytes 1114112 | tf_op jit(solution)/shard_map/jit(_take)/gather | solution.py:136
  104.7 1.1 select_bitcast_fusion
  105.9 9.1 %all-to-all-start.1 = ((f32[128,8,136]{2,1,0:T(8,128)}), f32[128,8,136]{2,1,0:T(8,128)S(1)}, u32[]{:S(2)}, u32[]{:S(2)}) async-start(f32[128,8,136]{2,1,0:T(8,128)} %select_bitcast_fusion), calls=%async_computation.1 | async-start | bytes 2097152 | tf_op jit(solution)/shard_map/all_to_all | solution.py:141
  115.0 0.3 convolution_bitcast_fusion.10
  115.4 0.3 convolution_bitcast_fusion.11
  115.7 0.4 multiply_reduce_fusion.9
  116.2 17.7 %all-to-all-done.1 = f32[128,8,136]{2,1,0:T(8,128)S(1)} async-done(((f32[128,8,136]{2,1,0:T(8,128)}), f32[128,8,136]{2,1,0:T(8,128)S(1)}, u32[]{:S(2)}, u32[]{:S(2)}) %all-to-all-start.1) | async-done | bytes 557088 | tf_op jit(solution)/shard_map/all_to_all | solution.py:141
  133.9 2.9 slice_reduce_fusion.6
  137.9 64.3 %scatter_custom_fusion = f32[6912]{0:T(1024)S(1)} fusion(s32[17408]{0:T(1024)} %bitcast.268, f32[17408]{0:T(1024)S(1)} %multiply_exponential_fusion, f32[]{:T(128)} %constant.313.clone.1), kind=kCustom, calls=%fused_computation.166 | custom fusion | bytes 28160 | tf_op jit(solution)/shard_map/scatter | solution.py:174
  202.3 0.5 multiply_reduce_fusion.8
  202.9 0.3 convolution_bitcast_fusion.28
  203.2 0.3 convolution_bitcast_fusion.26
  203.5 0.3 convolution_bitcast_fusion.25
  205.1 0.7 collective-permute-start.4
  205.8 6.3 %collective-permute-done.4 = f32[3,1,5,128]{3,1,2,0:T(1,128)S(1)} collective-permute-done((f32[3,1,5,128]{3,1,2,0:T(1,128)S(1)}, f32[3,1,5,128]{3,1,2,0:T(1,128)S(1)}, u32[]{:S(2)}, u32[]{:S(2)}) %collective-permute-start.4) | collective-permute-done | bytes 7712 | tf_op jit(solution)/shard_map/ppermute | solution.py:19
  212.3 3.6 collective-permute-done.5
  215.9 4.3 %collective-permute-done.6 = f32[3,5,1,128]{3,1,2,0:T(8,128)S(1)} collective-permute-done((f32[3,5,1,128]{3,1,2,0:T(8,128)S(1)}, f32[3,5,1,128]{3,1,2,0:T(8,128)S(1)}, u32[]{:S(2)}, u32[]{:S(2)}) %collective-permute-start.6) | collective-permute-done | bytes 7712 | tf_op jit(solution)/shard_map/ppermute | solution.py:19
  220.3 1.4 collective-permute-done.7
  222.7 0.3 convolution_bitcast_fusion.6
  223.0 0.3 convolution_bitcast_fusion.7
  223.4 0.3 convolution_bitcast_fusion.8
  223.7 0.7 multiply_reduce_fusion.5
  224.4 0.4 multiply_reduce_fusion.18
  224.8 0.8 fusion.37
  228.1 2.0 stack.121
  230.1 15.3 %psum.28 = f32[6]{0:T(128)S(1)} all-reduce(f32[6]{0:T(128)S(1)} %stack.121), channel_id=1, replica_groups=mesh['mesh'=16,'bg'=8] {'bg'}, use_global_device_ids=true, to_apply=%region_18.19 | all-reduce | flops 6 | bytes 48 | tf_op jit(solution)/shard_map/psum | solution.py:188
  245.4 39.0 %psum.29 = f32[6]{0:T(128)S(1)} all-reduce(f32[6]{0:T(128)S(1)} %psum.28), channel_id=1, replica_groups=mesh['mesh'=16,'bg'=8] {'mesh'}, use_global_device_ids=true, to_apply=%region_19.20 | all-reduce | flops 6 | bytes 48 | tf_op jit(solution)/shard_map/psum | solution.py:188
  284.4 0.7 fusion.60
  296.1 0.3 convolution_bitcast_fusion.3
  296.5 0.3 convolution_bitcast_fusion.4
  296.8 0.3 convolution_bitcast_fusion.5
  297.2 0.4 multiply_reduce_fusion.4
  297.7 0.5 multiply_reduce_fusion.3
  298.3 0.3 convolution_bitcast_fusion.18
  298.8 0.3 convolution_bitcast_fusion.15
  300.5 7.0 %collective-permute-done.8 = f32[3,1,5,128]{3,1,2,0:T(1,128)S(1)} collective-permute-done((f32[3,1,5,128]{3,1,2,0:T(1,128)S(1)}, f32[3,1,5,128]{3,1,2,0:T(1,128)S(1)}, u32[]{:S(2)}, u32[]{:S(2)}) %collective-permute-start.8) | collective-permute-done | bytes 7712 | tf_op jit(solution)/shard_map/ppermute | solution.py:19
  307.6 3.6 collective-permute-done.9
  311.3 4.3 %collective-permute-done.10 = f32[3,5,1,128]{3,1,2,0:T(8,128)S(1)} collective-permute-done((f32[3,5,1,128]{3,1,2,0:T(8,128)S(1)}, f32[3,5,1,128]{3,1,2,0:T(8,128)S(1)}, u32[]{:S(2)}, u32[]{:S(2)}) %collective-permute-start.10) | collective-permute-done | bytes 7712 | tf_op jit(solution)/shard_map/ppermute | solution.py:19
  315.6 1.4 collective-permute-done.11
  318.0 0.3 convolution_bitcast_fusion
  318.4 0.3 convolution_bitcast_fusion.1
  318.7 0.3 convolution_bitcast_fusion.2
  319.1 0.7 multiply_reduce_fusion
  319.7 0.4 multiply_reduce_fusion.12
  320.1 0.8 fusion.43
  323.5 2.0 stack.136
  325.5 15.3 %psum.30 = f32[6]{0:T(128)S(1)} all-reduce(f32[6]{0:T(128)S(1)} %stack.136), channel_id=1, replica_groups=mesh['mesh'=16,'bg'=8] {'bg'}, use_global_device_ids=true, to_apply=%region_37.38 | all-reduce | flops 6 | bytes 48 | tf_op jit(solution)/shard_map/psum | solution.py:188
  340.8 38.8 %psum.31 = f32[6]{0:T(128)S(1)} all-reduce(f32[6]{0:T(128)S(1)} %psum.30), channel_id=1, replica_groups=mesh['mesh'=16,'bg'=8] {'mesh'}, use_global_device_ids=true, to_apply=%region_38.39 | all-reduce | flops 6 | bytes 48 | tf_op jit(solution)/shard_map/psum | solution.py:188
  379.6 0.7 fusion.59
  390.2 0.6 copy.210
  390.9 0.6 pad_maximum_fusion.2
  (119 shorter events, 10.3 us)
Async XLA Ops:
  0.6 22.1 %copy-start.7 = (f32[6]{0:T(128)S(1)}, f32[6]{0:T(128)}, u32[]{:S(2)}) copy-start(f32[6]{0:T(128)} %constant.334.clone) | copy-start | bytes 76
  0.6 23.5 %copy-start.6 = (f32[192]{0:T(256)S(1)}, f32[192]{0:T(256)}, u32[]{:S(2)}) copy-start(f32[192]{0:T(256)} %constant.335.clone) | copy-start | bytes 2308
  0.7 16.9 %copy-start.5 = (f32[3,4,4,128]{3,2,1,0:T(4,128)S(1)}, f32[3,4,4,128]{3,2,1,0:T(4,128)}, u32[]{:S(2)}) copy-start(f32[3,4,4,128]{3,2,1,0:T(4,128)} %param.38) | copy-start | bytes 73732
  0.7 27.8 %copy-start.4 = (f32[8,16384]{1,0:T(8,128)S(1)}, f32[8,16384]{1,0:T(8,128)}, u32[]{:S(2)}) copy-start(f32[8,16384]{1,0:T(8,128)} %param.39) | copy-start | bytes 1572868
  0.7 16.9 %collective-permute-start = (f32[3,1,5,128]{3,1,2,0:T(1,128)S(1)}, f32[3,1,5,128]{3,1,2,0:T(1,128)S(1)}, u32[]{:S(2)}, u32[]{:S(2)}) collective-permute-start(f32[3,1,5,128]{3,1,2,0:T(1,128)S(1)} %slice.391), channel_id=1, source_target_pairs={{0,8},{8,16},{16,24},{24,32},{32,40},{40,48},{48,56},{56,64},{64,7... | collective-permute-start | bytes 23048 | tf_op jit(solution)/shard_map/ppermute | solution.py:19
  4.0 31.9 %all-to-all-start = ((s32[128,1,136]{2,1,0:T(1,128)}), s32[128,1,136]{2,1,0:T(1,128)S(1)}, u32[]{:S(2)}, u32[]{:S(2)}) async-start(s32[128,1,136]{2,1,0:T(1,128)} %bitcast.21), calls=%async_computation | async-start | bytes 262144 | tf_op jit(solution)/shard_map/all_to_all | solution.py:167
  17.6 6.4 %collective-permute-start.1 = (f32[3,1,5,128]{3,1,2,0:T(1,128)S(1)}, f32[3,1,5,128]{3,1,2,0:T(1,128)S(1)}, u32[]{:S(2)}, u32[]{:S(2)}) collective-permute-start(f32[3,1,5,128]{3,1,2,0:T(1,128)S(1)} %get-tuple-element.209), channel_id=1, source_target_pairs={{8,0},{16,8},{24,16},{32,24},{40,32},{48,40},{56,48},{64,56},{72,6... | collective-permute-start | bytes 23048 | tf_op jit(solution)/shard_map/ppermute | solution.py:22
  24.2 4.3 %collective-permute-start.2 = (f32[3,5,1,128]{3,1,2,0:T(8,128)S(1)}, f32[3,5,1,128]{3,1,2,0:T(8,128)S(1)}, u32[]{:S(2)}, u32[]{:S(2)}) collective-permute-start(f32[3,5,1,128]{3,1,2,0:T(8,128)S(1)} %slice.426), channel_id=1, source_target_pairs={{0,1},{1,2},{2,3},{3,4},{4,5},{5,6},{6,7},{7,0},{8,9},{9,10},{10,1... | collective-permute-start | bytes 23048 | tf_op jit(solution)/shard_map/ppermute | solution.py:19
  28.5 6.0 %collective-permute-start.3 = (f32[3,5,1,128]{3,1,2,0:T(8,128)S(1)}, f32[3,5,1,128]{3,1,2,0:T(8,128)S(1)}, u32[]{:S(2)}, u32[]{:S(2)}) collective-permute-start(f32[3,5,1,128]{3,1,2,0:T(8,128)S(1)} %get-tuple-element.207), channel_id=1, source_target_pairs={{1,0},{2,1},{3,2},{4,3},{5,4},{6,5},{7,6},{0,7},{9,8},{10,9},{11,1... | collective-permute-start | bytes 23048 | tf_op jit(solution)/shard_map/ppermute | solution.py:22
  28.5 6.0 %copy-start.3 = (f32[5,6,1,1]{0,1,3,2:T(8,128)S(1)}, f32[5,6,1,1]{0,1,3,2:T(8,128)}, u32[]{:S(2)}) copy-start(f32[5,6,1,1]{0,1,3,2:T(8,128)} %constant.344) | copy-start | bytes 364
  33.8 0.9 copy-start.2
  33.8 1.7 copy-start
  105.9 9.5 %copy-start.1 = (f32[128,192,1,1]{0,1,3,2:T(8,128)S(1)}, f32[128,192,1,1]{0,1,3,2:T(8,128)}, u32[]{:S(2)}) copy-start(f32[128,192,1,1]{0,1,3,2:T(8,128)} %constant.343) | copy-start | bytes 294916
  105.9 28.0 %all-to-all-start.1 = ((f32[128,8,136]{2,1,0:T(8,128)}), f32[128,8,136]{2,1,0:T(8,128)S(1)}, u32[]{:S(2)}, u32[]{:S(2)}) async-start(f32[128,8,136]{2,1,0:T(8,128)} %select_bitcast_fusion), calls=%async_computation.1 | async-start | bytes 2097152 | tf_op jit(solution)/shard_map/all_to_all | solution.py:141
  205.1 7.0 %collective-permute-start.4 = (f32[3,1,5,128]{3,1,2,0:T(1,128)S(1)}, f32[3,1,5,128]{3,1,2,0:T(1,128)S(1)}, u32[]{:S(2)}, u32[]{:S(2)}) collective-permute-start(f32[3,1,5,128]{3,1,2,0:T(1,128)S(1)} %slice.440), channel_id=1, source_target_pairs={{0,8},{8,16},{16,24},{24,32},{32,40},{40,48},{48,56},{56,64},{64,7... | collective-permute-start | bytes 23048 | tf_op jit(solution)/shard_map/ppermute | solution.py:19
  212.1 3.7 collective-permute-start.5
  215.9 4.3 %collective-permute-start.6 = (f32[3,5,1,128]{3,1,2,0:T(8,128)S(1)}, f32[3,5,1,128]{3,1,2,0:T(8,128)S(1)}, u32[]{:S(2)}, u32[]{:S(2)}) collective-permute-start(f32[3,5,1,128]{3,1,2,0:T(8,128)S(1)} %slice.443), channel_id=1, source_target_pairs={{0,1},{1,2},{2,3},{3,4},{4,5},{5,6},{6,7},{7,0},{8,9},{9,10},{10,1... | collective-permute-start | bytes 23048 | tf_op jit(solution)/shard_map/ppermute | solution.py:19
  220.3 1.4 collective-permute-start.7
  300.4 7.0 %collective-permute-start.8 = (f32[3,1,5,128]{3,1,2,0:T(1,128)S(1)}, f32[3,1,5,128]{3,1,2,0:T(1,128)S(1)}, u32[]{:S(2)}, u32[]{:S(2)}) collective-permute-start(f32[3,1,5,128]{3,1,2,0:T(1,128)S(1)} %slice.446), channel_id=1, source_target_pairs={{0,8},{8,16},{16,24},{24,32},{32,40},{40,48},{48,56},{56,64},{64,7... | collective-permute-start | bytes 23048 | tf_op jit(solution)/shard_map/ppermute | solution.py:19
  307.5 3.7 collective-permute-start.9
  311.3 4.3 %collective-permute-start.10 = (f32[3,5,1,128]{3,1,2,0:T(8,128)S(1)}, f32[3,5,1,128]{3,1,2,0:T(8,128)S(1)}, u32[]{:S(2)}, u32[]{:S(2)}) collective-permute-start(f32[3,5,1,128]{3,1,2,0:T(8,128)S(1)} %slice.449), channel_id=1, source_target_pairs={{0,1},{1,2},{2,3},{3,4},{4,5},{5,6},{6,7},{7,0},{8,9},{9,10},{10,1... | collective-permute-start | bytes 23048 | tf_op jit(solution)/shard_map/ppermute | solution.py:19
  315.6 1.4 collective-permute-start.11
